TPU v7x, 32 devices: a whole 2x2x4 slice. The times are simulated.
32 devices in a mesh: dp: 16 (over z, x, core), mp: 2 (over y).
Axes of the slice: x: 2, y: 2, z: 4, core: 2. Of those that a mesh axis runs over, the one named last changes fastest.
Arguments:
- inputs: bfloat16 [2, 16384, 768], P(None, ('dp', 'mp')), may hold values from -6 to 6
- roi_features: bfloat16 [2, 16384, 768], P(None, ('dp', 'mp')), may hold values from -6 to 6
- cotangent: bfloat16 [2, 16384, 768], P(None, ('dp', 'mp')), may hold values from -6 to 6
- doc_lengths: int32 [2, 16, 8], P(None, 'dp'), may hold values from 0 to 1024, as said below
- live_mask: int32 [2, 16384], P(None, 'dp'), may hold values 0 or 1
- bucket_cells: int32 [2, 3, 16384], P(None, None, 'dp'), may hold values from 0 to 31
- gain_attn: float32 [768], replicated, may hold values from 0.4 to 1.6
- gain_ffn: float32 [768], replicated, may hold values from 0.4 to 1.6
- w_query: bfloat16 [768, 768], P(None, 'mp'), may hold values from -0.21875 to 0.21875
- w_key: bfloat16 [768, 768], P(None, 'mp'), may hold values from -0.21875 to 0.21875
- w_value: bfloat16 [768, 768], P(None, 'mp'), may hold values from -0.21875 to 0.21875
- w_out: bfloat16 [768, 768], P('mp'), may hold values from -0.875 to 0.875
- w_up: bfloat16 [768, 3072], P(None, 'mp'), may hold values from -0.21875 to 0.21875
- w_down: bfloat16 [3072, 768], P('mp'), may hold values from -0.15625 to 0.15625
- bias_tables: float32 [3, 32, 12], P(None, None, 'mp'), may hold values from -4 to 4
Outputs:
- outputs: float32 [2, 16384, 768], P(None, ('dp', 'mp'))
- grad_inputs: float32 [2, 16384, 768], P(None, ('dp', 'mp'))
- grad_gain_attn: float32 [768], replicated
- grad_gain_ffn: float32 [768], replicated
- grad_w_query: float32 [768, 768], P(None, 'mp')
- grad_w_key: float32 [768, 768], P(None, 'mp')
- grad_w_value: float32 [768, 768], P(None, 'mp')
- grad_w_out: float32 [768, 768], P('mp')
- grad_w_up: float32 [768, 3072], P(None, 'mp')
- grad_w_down: float32 [3072, 768], P('mp')
- grad_bias_tables: float32 [3, 32, 12], P(None, None, 'mp')
Inputs may be any that keep to these rules, and one draw needn't show every extreme that they name: `doc_lengths`: each pack's 8 lengths sum to at most 1024; unused slots are 0; in every draw some pack is one document of 1024 tokens.
All inputs are finite; a program needn't handle non-finite values. No bound on the sum of `live_mask` on one device may be relied on, other than what follows from the above.
Results may differ from a plain program's by a relative error of at most 0.018.
Values may be sent and summed in bfloat16 or wider, within the bound.
A program may use at most 256 MiB of HBM per device.

v0:
```python
import functools
import math

import jax
import jax.numpy as jnp
from jax import lax
from jax.experimental import pallas as pl
from jax.experimental.pallas import tpu as pltpu
from jax.sharding import PartitionSpec as P

BF = jnp.bfloat16
F32 = jnp.float32
HDIM = 64
EPS = 1e-06
MASKED = -1e30
MESH = pl.DeviceIdType.MESH
VMEM = pl.BlockSpec(memory_space=pltpu.VMEM)
ANY = pl.BlockSpec(memory_space=pltpu.HBM)
SHAPE = jax.ShapeDtypeStruct


def dg(a, b, ca, cb):
    return lax.dot_general(a, b, (((ca,), (cb,)), ((), ())), preferred_element_type=F32)


def params(limit=58, **more):
    return pltpu.CompilerParams(vmem_limit_bytes=limit << 20, **more)


class Copy:
    def __init__(self, make):
        self.make = make

    def start(self):
        self.make().start()

    def wait(self):
        self.make().wait()

    def wait_recv(self):
        self.make().wait_recv()

    def wait_send(self):
        self.make().wait_send()


def now(ref):
    return ref() if callable(ref) else ref


class Links:
    def __init__(self, send, recv):
        self.send, self.recv, self.count = send, recv, 0
        self.d, self.m = lax.axis_index("dp"), lax.axis_index("mp")

    def flipped(self, dp_flip, mp_flip):
        dp = self.d ^ dp_flip if dp_flip else self.d
        mp = self.m ^ mp_flip if mp_flip else self.m
        return dp, mp

    def remote(self, src, dst, dp_flip=0, mp_flip=0):
        i = self.count
        self.count += 1
        return Copy(
            lambda: pltpu.make_async_remote_copy(
                src_ref=now(src),
                dst_ref=now(dst),
                send_sem=self.send.at[i],
                recv_sem=self.recv.at[i],
                device_id=self.flipped(dp_flip, mp_flip),
                device_id_type=MESH,
            )
        )

    def local(self, src, dst):
        i = self.count
        self.count += 1
        return Copy(lambda: pltpu.make_async_copy(now(src), now(dst), self.send.at[i]))

    def barrier(self, flips):
        sem = pltpu.get_barrier_semaphore()
        for flip in flips:
            pl.semaphore_signal(
                sem, inc=1, device_id=self.flipped(*flip), device_id_type=MESH
            )
        pl.semaphore_wait(sem, len(flips))


def rows_at(start, size, unit):
    return pl.ds(pl.multiple_of(start, unit), size)


def accumulate(into, other, start=0):
    n = into.shape[0]
    unit = 48 if n % 48 == 0 else 32

    def body(i, carry):
        here = rows_at(i * unit, unit, 16)
        there = rows_at(start + i * unit, unit, 16)
        into[here] = (into[here].astype(F32) + other[there].astype(F32)).astype(BF)
        return carry

    lax.fori_loop(0, n // unit, body, 0)


def carry_over(into, source, start=0):
    n = into.shape[0]
    unit = 48 if n % 48 == 0 else 32

    def body(i, carry):
        into[rows_at(i * unit, unit, 16)] = source[rows_at(start + i * unit, unit, 16)]
        return carry

    lax.fori_loop(0, n // unit, body, 0)


def entry_kernel(
    inp, roi, tab, gain, wq, wk, wv, wup,
    xf, tabo, wqkv, qt, kv, upo,
    sent, n1, send, recv,
):
    links = Links(send, recv)
    d, m = links.d, links.m
    rows = inp.shape[1]
    width, third = wq.shape
    piece = width // 8
    core, cross, deep = d & 1, (d >> 1) & 1, (d >> 2) & 1
    place = core * 4 + cross * 2 + deep
    links.barrier(((0, 1), (1, 0), (2, 0), (4, 0)))
    started = []

    def go(copy):
        copy.start()
        started.append(copy)
        return copy

    own_cols = [slice(j * third, (j + 1) * third) for j in range(3)]
    other_cols = [slice((3 + j) * third, (4 + j) * third) for j in range(3)]
    spot = rows_at(place * piece, piece, piece)
    first = [
        go(links.remote(w.at[spot], wqkv.at[spot, c], mp_flip=1))
        for w, c in zip((wq, wk, wv), other_cols)
    ]
    tab_copy = go(links.remote(tab, tabo, mp_flip=1))
    chunk = rows // 2
    row_copies = []
    for j in range(2):
        part = slice(j * chunk, (j + 1) * chunk)
        sent[part] = (inp[1 - m, part].astype(F32) + roi[1 - m, part].astype(F32)).astype(BF)
        here = rows_at(m * rows + j * chunk, chunk, chunk)
        row_copies.append(go(links.remote(sent.at[part], xf.at[here], mp_flip=1)))
    up_copy = go(links.remote(wup.at[spot], upo.at[spot], mp_flip=1))
    for w, c in zip((wq, wk, wv), own_cols):
        wqkv[:, c] = w[...]

    def normalise(where):
        x = xf[where].astype(F32)
        inverse = lax.rsqrt(jnp.mean(x * x, axis=-1, keepdims=True) + EPS)
        n1[where] = (x * inverse * gain[...]).astype(BF)

    own = rows_at(m * rows, rows, rows)
    xf[own] = (inp[m].astype(F32) + roi[m].astype(F32)).astype(BF)
    normalise(own)

    def project(where, side):
        rows_in = n1[where]
        base = side * 3 * third
        kv[where, side * 2 * third : (side + 1) * 2 * third] = dg(
            rows_in, wqkv[:, base + third : base + 3 * third], 1, 0
        ).astype(BF)
        qt[side * third : (side + 1) * third, where] = dg(
            wqkv[:, base : base + third], rows_in, 0, 1
        ).astype(BF)

    project(own, 0)
    stage = first
    for flip, begin, count in (
        (4, place, 1),
        (2, core * 4 + cross * 2, 2),
        (1, core * 4, 4),
    ):
        for copy in stage:
            copy.wait_recv()
        there = wqkv.at[rows_at(begin * piece, count * piece, piece), 3 * third : 6 * third]
        stage = [go(links.remote(there, there, dp_flip=flip))]
    for j in range(2):
        row_copies[j].wait_recv()
        here = rows_at((1 - m) * rows + j * chunk, chunk, chunk)
        normalise(here)
        project(here, 0)
    for copy in stage:
        copy.wait_recv()
    for j in range(2):
        project(slice(j * rows, (j + 1) * rows), 1)
    tab_copy.wait_recv()
    up_copy.wait_recv()
    for copy in started:
        copy.wait_send()


def entry(inputs, roi, tab, gain, wq, wk, wv, wup):
    rows, width = inputs.shape[1], inputs.shape[2]
    third = wq.shape[1]
    tokens = 2 * rows
    return pl.pallas_call(
        entry_kernel,
        out_shape=[
            SHAPE((tokens, width), BF),
            SHAPE(tab.shape, F32),
            SHAPE((width, 6 * third), BF),
            SHAPE((2 * third, tokens), BF),
            SHAPE((tokens, 4 * third), BF),
            SHAPE(wup.shape, BF),
        ],
        in_specs=[VMEM] * 7 + [ANY],
        out_specs=[VMEM] * 5 + [ANY],
        scratch_shapes=[
            pltpu.VMEM((rows, width), BF),
            pltpu.VMEM((tokens, width), BF),
            pltpu.SemaphoreType.DMA((12,)),
            pltpu.SemaphoreType.DMA((12,)),
        ],
        compiler_params=params(58, collective_id=1, has_side_effects=True),
        name="entry",
    )(inputs, roi, tab, gain, wq, wk, wv, wup)


def attend_kernel(
    lengths, live, cells, tab, tabo, qt_ref, k_ref, v_ref, cot, wo, wup, wdn, upo_in,
    p_ref, o_ref, r_ref, hot_ref, back_ref, dyo, woo, upo, dno,
    kx, qx, vx, mask, mats, hott_ref, send, recv, *, buckets,
):
    links = Links(send, recv)
    d, m = links.d, links.m
    tokens = k_ref.shape[0]
    rows = tokens // 2
    width, hidden = wup.shape
    inner = wo.shape[0]
    step = pl.program_id(0)
    core, cross, deep = d & 1, (d >> 1) & 1, (d >> 2) & 1
    place = core * 4 + cross * 2 + deep

    def block(full, begin, count):
        piece = full.shape[0] // 8
        return full.at[rows_at(begin * piece, count * piece, piece)]

    up = functools.partial(block, upo)
    down = functools.partial(block, dno)
    out = functools.partial(block, woo)
    dpiece, opiece = hidden // 8, inner // 8
    quarter = core * 4 + deep * 2
    down_y = links.remote(
        wdn.at[rows_at(quarter * dpiece, 2 * dpiece, dpiece)], down(quarter, 2), mp_flip=1
    )
    out_y = links.remote(wo.at[rows_at(place * opiece, opiece, opiece)], out(place, 1), mp_flip=1)
    dy_y = links.remote(cot.at[1 - m], dyo, mp_flip=1)
    up_z = links.remote(up(place, 1), up(place, 1), dp_flip=4)
    pair = core * 4 + cross * 2
    up_x = links.remote(up(pair, 2), up(pair, 2), dp_flip=2)
    up_c = links.remote(up(core * 4, 4), up(core * 4, 4), dp_flip=1)
    down_z = links.remote(down(quarter, 2), down(quarter, 2), dp_flip=4)
    down_c = links.remote(down(core * 4, 4), down(core * 4, 4), dp_flip=1)
    out_z = links.remote(out(place, 1), out(place, 1), dp_flip=4)
    out_x = links.remote(out(pair, 2), out(pair, 2), dp_flip=2)
    out_c = links.remote(out(core * 4, 4), out(core * 4, 4), dp_flip=1)

    def slot0():
        links.barrier(((0, 1), (1, 0), (2, 0), (4, 0)))
        up_z.start()
        down_y.start()
        out_y.start()
        dy_y.start()

    def slot4():
        up_z.wait_recv()
        up_x.start()

    def slot6():
        out_y.wait_recv()
        out_z.start()

    def slot7():
        down_y.wait_recv()
        down_z.start()

    def slot9():
        out_z.wait_recv()
        out_x.start()

    def slot11():
        up_x.wait_recv()
        up_c.start()
        out_x.wait_recv()
        out_c.start()

    def last():
        down_z.wait_recv()
        down_c.start()
        for copy in (dy_y, up_c, out_c, down_c):
            copy.wait_recv()
        for copy in (down_y, out_y, dy_y, up_z, up_x, up_c, down_z, down_c, out_z, out_x, out_c):
            copy.wait_send()

    slots = {0: slot0, 4: slot4, 6: slot6, 7: slot7, 9: slot9, 11: slot11}

    @pl.when(step == 0)
    def _():
        slot0()
        vx[64:80, :] = jnp.ones((16, tokens), BF)
        lane = lax.broadcasted_iota(jnp.int32, (buckets, tokens), 0)
        for t in range(3):
            row = cells[m, t : t + 1, :]
            hott_ref[t * buckets : (t + 1) * buckets, :] = jnp.where(row == lane, 1.0, 0.0).astype(BF)
            mirror = jnp.where(row == buckets - 1 - lane, 1.0, 0.0).astype(BF)
            back_ref[t * buckets : (t + 1) * buckets, :] = mirror
        hott_ref[96:128, :] = jnp.zeros((32, tokens), BF)
        wide_hot = hott_ref[...].T
        hot_ref[...] = wide_hot
        hot = wide_hot[:, 0:96]
        kx[:, 64:160] = hot
        kx[:, 160:256] = hot
        row_ids = lax.broadcasted_iota(jnp.int32, (1, tokens), 1)
        col_ids = lax.broadcasted_iota(jnp.int32, (tokens, 1), 0)
        seg_row = jnp.zeros((1, tokens), jnp.int32)
        seg_col = jnp.zeros((tokens, 1), jnp.int32)
        end = 0
        for i in range(lengths.shape[2]):
            end = end + lengths[m, 0, i]
            seg_row = seg_row + jnp.where(row_ids >= end, 1, 0)
            seg_col = seg_col + jnp.where(col_ids >= end, 1, 0)
        live_row = live[m].astype(F32)
        live_col = jnp.broadcast_to(live_row, (8, tokens)).T[:, 0:1]
        code = jnp.where(live_col == 1.0, seg_col, -1)
        allowed = (code == seg_row) | (col_ids == row_ids)
        mask[...] = jnp.where(allowed, 0.0, MASKED)
        line = lax.broadcasted_iota(jnp.int32, (128, 128), 0)
        lane = lax.broadcasted_iota(jnp.int32, (128, 128), 1)
        shift = jnp.where(lane < 64, lane, lane - 128)
        bucket = jnp.clip(-shift, -(buckets // 2), buckets // 2 - 1) + buckets // 2
        side = lax.broadcasted_iota(jnp.int32, (buckets, 128), 1)
        heads = mats.shape[0] // 2
        for part, table in enumerate((tab, tabo)):
            exact = table[...]
            upper = exact.astype(BF)
            lower = (exact - upper.astype(F32)).astype(BF)
            for t in range(3):
                pick = jnp.where(line == bucket + t * buckets, 1.0, 0.0).astype(BF)
                inside = (side >= t * buckets) & (side < (t + 1) * buckets)
                for level, source in enumerate((upper, lower)):
                    lines = dg(source, pick, 1, 0)
                    for h in range(heads):
                        wide = jnp.broadcast_to(lines[h : h + 1], (buckets, 128))
                        rolled = pltpu.roll(wide, t * buckets, 1, stride=1, stride_axis=0)
                        begin = level * 3 * buckets + t * buckets
                        mats[part * heads + h, begin : begin + buckets, :] = jnp.where(
                            inside, rolled, 0.0
                        ).astype(BF)

    vt = v_ref[...].T
    for h in range(2):
        for at, action in slots.items():
            if at % 2 == h and at > 0:
                pl.when(step == at // 2)(action)
        span = slice(64 * h, 64 * h + 64)
        kx[:, 0:64] = k_ref[:, span]
        qx[0:64, :] = qt_ref[span, :] * BF(0.125)
        qx[64:256, :] = dg(mats[2 * step + h], hott_ref[...], 1, 0).astype(BF)
        vx[0:64, :] = vt[span, :]
        s = dg(kx[...], qx[...], 1, 0) + mask[...]
        top = jnp.max(s, axis=0, keepdims=True)
        p = jnp.exp(s - top).astype(BF)
        p_ref[h] = p
        o = dg(vx[...], p, 1, 0)
        r = 1.0 / o[64:65, :]
        o_ref[span, :] = (o[0:64] * r).astype(BF)
        r_ref[0, h : h + 1, :] = r
    pl.when(step == pl.num_programs(0) - 1)(last)


def attend(lengths, live, cells, tab, tabo, qt, kv, cot, wo, wup, wdn, upo, buckets):
    channels, tokens = qt.shape
    width, hidden = wup.shape
    inner = wo.shape[0]
    pairs = channels // 128
    half = pairs // 2
    whole = lambda shape: pl.BlockSpec(shape, lambda i: (0,) * len(shape))
    return pl.pallas_call(
        functools.partial(attend_kernel, buckets=buckets),
        grid=(pairs,),
        in_specs=[
            pl.BlockSpec(memory_space=pltpu.SMEM),
            whole(live.shape),
            whole(cells.shape),
            whole(tab.shape),
            whole(tabo.shape),
            pl.BlockSpec((128, tokens), lambda i: (i, 0)),
            pl.BlockSpec((tokens, 128), lambda i: (0, (i // half) * 2 * half + i % half)),
            pl.BlockSpec((tokens, 128), lambda i: (0, (i // half) * 2 * half + half + i % half)),
            ANY, ANY, ANY, ANY, ANY,
        ],
        out_specs=[
            pl.BlockSpec((2, tokens, tokens), lambda i: (i, 0, 0)),
            pl.BlockSpec((128, tokens), lambda i: (i, 0)),
            pl.BlockSpec((1, 2, tokens), lambda i: (i, 0, 0)),
            whole((tokens, 128)),
            whole((96, tokens)),
            ANY, ANY, ANY, ANY,
        ],
        out_shape=[
            SHAPE((2 * pairs, tokens, tokens), BF),
            SHAPE((channels, tokens), BF),
            SHAPE((pairs, 2, tokens), F32),
            SHAPE((tokens, 128), BF),
            SHAPE((96, tokens), BF),
            SHAPE((tokens // 2, width), BF),
            SHAPE((inner, width), BF),
            SHAPE((width, hidden), BF),
            SHAPE((hidden, width), BF),
        ],
        input_output_aliases={12: 7},
        scratch_shapes=[
            pltpu.VMEM((tokens, 256), BF),
            pltpu.VMEM((256, tokens), BF),
            pltpu.VMEM((80, tokens), BF),
            pltpu.VMEM((tokens, tokens), F32),
            pltpu.VMEM((2 * pairs, 192, 128), BF),
            pltpu.VMEM((128, tokens), BF),
            pltpu.SemaphoreType.DMA((20,)),
            pltpu.SemaphoreType.DMA((20,)),
        ],
        compiler_params=params(58, collective_id=3, has_side_effects=True),
        name="attend",
    )(lengths, live, cells, tab, tabo, qt, kv, kv, cot, wo, wup, wdn, upo)


def middle_kernel(
    x_ref, mixt_ref, wo_in, woo_in, cot, dyo, gain_ref, wup_in, upo_in, wdn_in, dno_in,
    y_ref, gwo_ref, dh_ref, dmt_ref, gg_ref,
    sum1u, sum1d, sum2u, sum2d, own3u, own3d, far3u, far3d,
    h1, n2, n2t, yacc, dn, wo_ref, dy_ref, gu, gd, rcu, rcd, ryu, ryd, send, recv,
):
    links = Links(send, recv)
    core = links.d & 1
    step = pl.program_id(0)
    last = pl.num_programs(0) - 1
    half_steps = pl.num_programs(0) // 2
    early = step < half_steps
    width, chunk = gu.shape[1:]
    keep_u, give_u = (rows_at(c * (width // 2), width // 2, 16) for c in (core, 1 - core))
    keep_d, give_d = (rows_at(c * (chunk // 2), chunk // 2, 16) for c in (core, 1 - core))

    def core_copies(i):
        return (
            pltpu.make_async_remote_copy(
                gu.at[i % 2, give_u], rcu.at[i], send.at[0, i], recv.at[0, i],
                device_id=(links.d ^ 1, links.m), device_id_type=MESH,
            ),
            pltpu.make_async_remote_copy(
                gd.at[i % 2, give_d], rcd.at[i], send.at[1, i], recv.at[1, i],
                device_id=(links.d ^ 1, links.m), device_id_type=MESH,
            ),
        )

    def pair_copies(i):
        return (
            pltpu.make_async_remote_copy(
                rcu.at[i], ryu.at[i], send.at[2, i], recv.at[2, i],
                device_id=(links.d, 1 - links.m), device_id_type=MESH,
            ),
            pltpu.make_async_remote_copy(
                rcd.at[i], ryd.at[i], send.at[3, i], recv.at[3, i],
                device_id=(links.d, 1 - links.m), device_id_type=MESH,
            ),
        )

    def settle(i):
        for copy in core_copies(i):
            copy.wait_recv()
        for copy in core_copies(i):
            copy.wait_send()
        accumulate(rcu.at[i], gu.at[i % 2], core * (width // 2))
        accumulate(rcd.at[i], gd.at[i % 2], core * (chunk // 2))

    @pl.when(step == 0)
    def _():
        links.barrier(((0, 1), (1, 0)))
        m = links.m
        rows = dyo.shape[0]
        dy_ref[rows_at(m * rows, rows, rows)] = cot[m]
        dy_ref[rows_at((1 - m) * rows, rows, rows)] = dyo[...]
        inner = wo_in.shape[0]
        wo_ref[0:inner] = wo_in[...]
        wo_ref[inner:] = woo_in[...]
        added = dg(mixt_ref[...], wo_ref[...], 0, 0)
        h = x_ref[...].astype(F32) + added
        h1[...] = h
        yacc[...] = added
        inverse = lax.rsqrt(jnp.mean(h * h, axis=-1, keepdims=True) + EPS)
        normed = (h * inverse * gain_ref[...]).astype(BF)
        n2[...] = normed
        n2t[...] = normed.T
        dn[...] = jnp.zeros_like(dn)

    wup = jnp.where(early, upo_in[...], wup_in[...])
    wdn = jnp.where(early, dno_in[...], wdn_in[...])
    dy = dy_ref[...]
    u = dg(n2[...], wup, 1, 0)
    cdf = 0.5 * (1.0 + lax.erf(u * 0.7071067811865476))
    act = (u * cdf).astype(BF)
    grad_act = dg(dy, wdn, 1, 1)
    density = jnp.exp(u * u * (-0.5)) * 0.3989422804014327
    du = (grad_act * (cdf + u * density)).astype(BF)
    yacc[...] += dg(act, wdn, 1, 0)

    @pl.when(step > 0)
    def _():
        settle(step - 1)

    @pl.when((step > 0) & (step < half_steps))
    def _():
        for copy in pair_copies(step - 1):
            copy.start()

    dn[...] += dg(du, wup, 1, 1)
    gu[step % 2] = dg(n2t[...], du, 1, 0).astype(BF)
    gd[step % 2] = dg(act, dy, 0, 0).astype(BF)
    for copy in core_copies(step):
        copy.start()

    @pl.when(step == last)
    def _():
        h = h1[...]
        inverse = lax.rsqrt(jnp.mean(h * h, axis=-1, keepdims=True) + EPS)
        normed = h * inverse
        grad = dn[...]
        gg_ref[...] = jnp.sum(grad * normed, axis=0, keepdims=True)
        inner = grad * gain_ref[...]
        added = inverse * (inner - normed * jnp.mean(inner * normed, axis=-1, keepdims=True))
        dh_ref[...] = added
        y_ref[...] = yacc[...].astype(BF)
        low = (dy_ref[...].astype(F32) + added).astype(BF)
        gwo_ref[...] = dg(low, mixt_ref[...], 0, 1).astype(BF)
        dmt_ref[...] = dg(wo_ref[...], low, 1, 1).astype(BF)
        settle(last)
        n = rcu.shape[0] // 2
        for k, (out_u, out_d) in enumerate(((sum1u, sum1d), (sum2u, sum2d))):
            for copy in pair_copies(k):
                copy.wait_recv()
            accumulate(rcu.at[n + k], ryu.at[k])
            accumulate(rcd.at[n + k], ryd.at[k])
            carry_over(out_u, rcu.at[n + k])
            carry_over(out_d, rcd.at[n + k])
        carry_over(own3u, rcu.at[n + 2])
        carry_over(own3d, rcd.at[n + 2])
        carry_over(far3u, rcu.at[2])
        carry_over(far3d, rcd.at[2])
        for k in range(2):
            for copy in pair_copies(k):
                copy.wait_send()


def middle(x, mixt, wo, woo, cot, dyo, gain, wup, upo, wdn, dno):
    tokens, width = x.shape
    half = wup.shape[1]
    chunk = half // 3
    n = 6
    once = lambda shape: pl.BlockSpec(
        shape, lambda i: (0,) * len(shape), pipeline_mode=pl.Buffered(1)
    )
    late = lambda i: jnp.maximum(i - n // 2, 0)
    early = lambda i: jnp.minimum(i, n // 2 - 1)
    part_u, part_d = (width // 2, chunk), (chunk // 2, width)
    outs = [
        ((tokens, width), BF),
        ((width, width), BF),
        ((tokens, width), F32),
        ((width, tokens), BF),
        ((1, width), F32),
    ] + [(part_u, BF), (part_d, BF)] * 4
    return pl.pallas_call(
        middle_kernel,
        grid=(n,),
        in_specs=[
            once((tokens, width)),
            once((width, tokens)),
            once(wo.shape),
            once(woo.shape),
            once(cot.shape),
            once(dyo.shape),
            once((1, width)),
            pl.BlockSpec((width, chunk), lambda i: (0, late(i))),
            pl.BlockSpec((width, chunk), lambda i: (0, early(i))),
            pl.BlockSpec((chunk, width), lambda i: (late(i), 0)),
            pl.BlockSpec((chunk, width), lambda i: (early(i), 0)),
        ],
        out_specs=[once(shape) for shape, _ in outs],
        out_shape=[SHAPE(*entry) for entry in outs],
        scratch_shapes=[
            pltpu.VMEM((tokens, width), F32),
            pltpu.VMEM((tokens, width), BF),
            pltpu.VMEM((width, tokens), BF),
            pltpu.VMEM((tokens, width), F32),
            pltpu.VMEM((tokens, width), F32),
            pltpu.VMEM((width, width), BF),
            pltpu.VMEM((tokens, width), BF),
            pltpu.VMEM((2, width, chunk), BF),
            pltpu.VMEM((2, chunk, width), BF),
            pltpu.VMEM((n,) + part_u, BF),
            pltpu.VMEM((n,) + part_d, BF),
            pltpu.VMEM((2,) + part_u, BF),
            pltpu.VMEM((2,) + part_d, BF),
            pltpu.SemaphoreType.DMA((4, n)),
            pltpu.SemaphoreType.DMA((4, n)),
        ],
        compiler_params=params(60, collective_id=4, has_side_effects=True),
        name="middle",
    )(x, mixt, wo, woo, cot, dyo, gain, wup, upo, wdn, dno)


class Unit:
    def __init__(self, links, n, w, rx, rz, zp, final, far, n_dp, deepest):
        self.links, self.n, self.w = links, n, w
        self.rx, self.rz, self.zp, self.final, self.far = rx, rz, zp, final, far
        self.n_dp, self.stepwise = n_dp, deepest
        d = links.d
        self.core, self.cross = d & 1, (d >> 1) & 1
        self.b0, self.b1 = (d >> 2) & 1, (d >> 3) & 1
        q = n // 16
        self.q = q
        self.xr = links.remote(lambda: self.xr.make_source(), rx, dp_flip=2)
        spot = self.core * 8 + self.cross * 4 + self.b0 * 2 + self.b1
        self.piece = lambda: final(spot * q, q)
        self.home = links.local(zp, self.piece)
        if deepest:
            keep = self.b0 * 2
            give = (1 - self.b0) * 2
            self.z1 = links.remote(lambda: rx.at[rows_at(give * q, 2 * q, 16)], rz[0], dp_flip=4)
            self.z2 = links.remote(
                lambda: rz[0].at[rows_at((1 - self.b1) * q, q, 16)], rz[1], dp_flip=8
            )
            self.g2 = links.remote(zp, self.piece, dp_flip=8)
            both = lambda: final((self.core * 8 + self.cross * 4 + keep) * q, 2 * q)
            self.g1 = links.remote(both, both, dp_flip=4)
        else:
            self.zs, self.gs = [], []
            for r in range(1, 4):
                p0, p1 = self.b0 ^ (r & 1), self.b1 ^ (r >> 1)
                src = lambda p=p0 * 2 + p1: rx.at[rows_at(p * q, q, 16)]
                dst = lambda r=r: rz[0].at[r - 1]
                self.zs.append(links.remote(src, dst, dp_flip=r << 2))
                self.gs.append(links.remote(zp, self.piece, dp_flip=r << 2))
        quad = lambda: final((self.core * 8 + self.cross * 4) * q, 4 * q)
        self.gx = links.remote(quad, quad, dp_flip=2)
        side = lambda: final(self.core * 8 * q, 8 * q)
        self.gc = links.remote(side, side, dp_flip=1)
        if far is not None:
            self.others = [
                links.remote(lambda: far.at[0], lambda r=r: far.at[r], dp_flip=r << 4)
                for r in range(1, n_dp // 16)
            ]

    def start_x(self, source):
        half = self.n // 4
        self.xr.make_source = lambda: now(source).at[rows_at((1 - self.cross) * half, half, 16)]
        self.xr.start()

    def add_x(self, kept):
        half = self.n // 4
        self.xr.wait_recv()
        accumulate(self.rx, now(kept), self.cross * half)

    def start_z(self, kept):
        self.add_x(kept)
        for copy in [self.z1] if self.stepwise else self.zs:
            copy.start()

    def start_z2(self):
        self.z1.wait_recv()
        accumulate(self.rz[0], self.rx, self.b0 * 2 * self.q)
        self.z2.start()

    def start_back(self):
        q = self.q
        if self.stepwise:
            self.z2.wait_recv()
            total = self.rz[0][rows_at(self.b1 * q, q, 16)].astype(F32)
            total = total + self.rz[1][...].astype(F32)
        else:
            for copy in self.zs:
                copy.wait_recv()
            total = self.rx[rows_at((self.b0 * 2 + self.b1) * q, q, 16)].astype(F32)
            for r in range(3):
                total = total + self.rz[0][r].astype(F32)
        if self.far is not None:
            self.far[0] = total.astype(BF)
            for copy in self.others:
                copy.start()
            for r, copy in enumerate(self.others):
                copy.wait_recv()
                total = total + self.far[r + 1].astype(F32)
        self.zp[...] = total.astype(BF)
        self.home.start()
        for copy in [self.g2] if self.stepwise else self.gs:
            copy.start()

    def start_back1(self):
        self.home.wait()
        self.g2.wait_recv()
        self.g1.start()

    def start_back_x(self):
        if self.stepwise:
            self.g1.wait_recv()
        else:
            self.home.wait()
            for copy in self.gs:
                copy.wait_recv()
        self.gx.start()

    def start_back_c(self):
        self.gx.wait_recv()
        self.gc.start()

    def end(self):
        self.gc.wait_recv()
        sent = [self.xr, self.gx, self.gc]
        sent += [self.z1, self.z2, self.g2, self.g1] if self.stepwise else self.zs + self.gs
        if self.far is not None:
            sent += self.others
        for copy in sent:
            copy.wait_send()


def back_kernel(
    p_ref, qt_ref, k_ref, v_ref, ot_ref, dot_ref, r_ref, back_ref, hot_ref,
    x_ref, gain_ref, dh_ref, ggf_ref, wq_ref, wk_ref, wv_ref,
    sum1u, sum1d, sum2u, sum2d, own3u, own3d, far3u, far3d, gwo, y,
    yret, gret, fqkv, fwo, fup, fdn, small,
    vx, dox, kht, n1t, dn, gtab, gp, rcp, ryp, gin,
    k1u, k1d, k2u, k2d, k3u, k3d, ry3u, ry3d, kw, rcw, ryw,
    sums, got, *rest, n_dp, buckets,
):
    units_scratch, rest = rest[: 4 * 10], rest[4 * 10 :]
    far = rest[:10] if n_dp > 16 else [None] * 10
    send, recv = rest[-2:]
    links = Links(send, recv)
    d, m = links.d, links.m
    core = d & 1
    step = pl.program_id(0)
    tokens, width = x_ref.shape
    rows = tokens // 2
    chunk = far3u.shape[1]
    group = gp.shape[2]
    bits = n_dp.bit_length() - 1

    def region(ref, row0, col0, w, lead=None):
        def at(start, count):
            where = rows_at(row0 + start, count, 16)
            if lead is not None:
                return ref.at[lead, where]
            return ref.at[where, col0 : col0 + w]

        return at

    finals = []
    for k in range(3):
        finals.append((width, chunk, region(fup, 0, k * chunk, chunk), True))
        finals.append((chunk, width, region(fdn, k * chunk, 0, width), True))
    finals.append((width, group, region(fwo, 0, 0, group), False))
    for k in range(3):
        finals.append((width, group, region(fqkv, 0, 0, group, lead=k), False))
    units = []
    for i, (n, w, final, deepest) in enumerate(finals):
        rx, zp = units_scratch[4 * i], units_scratch[4 * i + 1]
        rz = units_scratch[4 * i + 2 : 4 * i + 4]
        units.append(Unit(links, n, w, rx, rz, zp, final, far[i], n_dp, deepest))
    ff = (units[0:2], units[2:4], units[4:6])
    wo, pairs = units[6], units[7:10]
    kept = ((k1u, k1d), (k2u, k2d), (ry3u, ry3d))
    heads_half = width // 2

    mine = rows_at(m * rows, rows, rows)
    theirs = rows_at((1 - m) * rows, rows, rows)
    y_home = links.local(lambda: y.at[mine], lambda: yret.at[m])
    y_away = links.remote(lambda: y.at[theirs], lambda: yret.at[m], mp_flip=1)
    gin_home = links.local(lambda: gin.at[mine], lambda: gret.at[m])
    gin_away = links.remote(lambda: gin.at[theirs], lambda: gret.at[m], mp_flip=1)
    loads = [
        links.local(src, dst)
        for src, dst in ((sum1u, k1u), (sum1d, k1d), (sum2u, k2u), (sum2d, k2d), (own3u, k3u), (own3d, k3d))
    ]
    keep = rows_at(core * (width // 2), width // 2, 16)
    give = rows_at((1 - core) * (width // 2), width // 2, 16)
    load_w = links.local(lambda: gwo.at[keep], kw)
    y3 = [links.remote(far3u, ry3u, mp_flip=1), links.remote(far3d, ry3d, mp_flip=1)]
    wo_c = links.remote(lambda: gwo.at[give], rcw, dp_flip=1)
    wo_y = links.remote(lambda: rcw.at[:, heads_half:], ryw, mp_flip=1)
    pair_c = [
        links.remote(lambda i=i: gp.at[i, give], lambda i=i: rcp.at[i], dp_flip=1) for i in range(6)
    ]
    pair_y = [
        links.remote(lambda i=i: rcp.at[i], lambda i=i: ryp.at[i], mp_flip=1) for i in range(3)
    ]

    def settle(i):
        pair_c[i].wait_recv()
        accumulate(rcp.at[i], gp.at[i], core * (width // 2))

    def send_other(i):
        settle(i)
        pair_y[i].start()

    def join_own(k):
        settle(3 + k)
        pair_y[k].wait_recv()
        accumulate(ryp.at[k], rcp.at[3 + k])
        pairs[k].start_x(lambda: ryp.at[k])

    def each(group_of, name, *args):
        for unit in group_of:
            getattr(unit, name)(*args)

    def ff_z(k):
        for unit, held in zip(ff[k], kept[k]):
            unit.start_z(held)

    def slot_start():
        links.barrier(
            [(0, 1)]
            + [(1 << b, 0) for b in range(bits)]
            + [(12, 0)]
            + [(r << 4, 0) for r in range(1, n_dp // 16) if r & (r - 1)]
        )
        for copy in loads:
            copy.start()
        load_w.start()
        wo_c.start()
        for copy in y3:
            copy.start()
        for unit, source in zip(ff[0], (sum1u, sum1d)):
            unit.start_x(source)
        for unit, source in zip(ff[1], (sum2u, sum2d)):
            unit.start_x(source)
        y_home.start()

    def slot_end(i):
        pair_c[i].start()
        if i == 0:
            load_w.wait()
            wo_c.wait_recv()
            accumulate(rcw, kw)
            wo_y.start()
            for copy in loads:
                copy.wait()
        if i == 1:
            ff_z(0)
            send_other(0)
        if i == 2:
            each(ff[0], "start_z2")
            ff_z(1)
            send_other(1)
            for unit, copy, held, own in zip(ff[2], y3, kept[2], (k3u, k3d)):
                copy.wait_recv()
                accumulate(held, own)
                unit.start_x(held)
        if i == 3:
            each(ff[0], "start_back")
            each(ff[1], "start_z2")
            send_other(2)
            y_away.start()
            wo_y.wait_recv()
            accumulate(ryw, rcw.at[:, 0:heads_half])
            wo.start_x(ryw)
        if i == 4:
            each(ff[0], "start_back1")
            each(ff[1], "start_back")
            ff_z(2)
            join_own(0)
            wo.start_z(ryw)
        if i == 5:
            each(ff[0], "start_back_x")
            each(ff[1], "start_back1")
            each(ff[2], "start_z2")
            join_own(1)
            wo.start_back()
            pairs[0].start_z(lambda: ryp.at[0])

    @pl.when(step == 0)
    def _():
        slot_start()
        kht[64:160, :] = back_ref[...]
        lanes = lax.broadcasted_iota(jnp.int32, (tokens, 64), 1)
        vx[:, 64:128] = jnp.where(lanes < 2, -1.0, 0.0).astype(BF)
        dox[64:128, :] = jnp.zeros((64, tokens), BF)
        x = x_ref[...].astype(F32)
        inverse = lax.rsqrt(jnp.mean(x * x, axis=-1, keepdims=True) + EPS)
        n1t[...] = (x * inverse * gain_ref[...]).astype(BF).T
        dn[...] = jnp.zeros_like(dn)
        gtab[...] = jnp.zeros_like(gtab)

    side = lax.broadcasted_iota(jnp.int32, (buckets, 128), 1)
    first_row = jnp.where(step < 3, 8 + 2 * step, 2 * (step - 3))
    dqs, dks, dvs = [], [], []
    for h in range(2):
        span = slice(64 * h, 64 * h + 64)
        scaled = dot_ref[span, :].astype(F32) * r_ref[0, h : h + 1, :]
        inner = jnp.sum(scaled * ot_ref[span, :].astype(F32), axis=0, keepdims=True)
        upper = inner.astype(BF)
        lower = (inner - upper.astype(F32)).astype(BF)
        dox[0:64, :] = scaled.astype(BF)
        dox[64:66, :] = jnp.concatenate([upper, lower], 0)
        vx[:, 0:64] = v_ref[:, span]
        kht[0:64, :] = k_ref[:, span].T
        dp = dg(vx[...], dox[...], 1, 0)
        p = p_ref[h]
        ds = (p.astype(F32) * dp).astype(BF)
        dvs.append(dg(p, dox[0:64, :], 1, 1).astype(BF))
        dks.append((dg(ds, qt_ref[span, :], 1, 1) * 0.125).astype(BF))
        both = dg(kht[...], ds, 1, 0)
        dqs.append((both[0:64] * 0.125).astype(BF).T)
        left = both[64:160]
        left_hi = left.astype(BF)
        left_lo = (left - left_hi.astype(F32)).astype(BF)
        hot = hot_ref[...]
        blocks = dg(left_hi, hot, 1, 0) + dg(left_lo, hot, 1, 0)
        for t in range(3):
            inside = (side >= t * buckets) & (side < (t + 1) * buckets)
            block = jnp.where(inside, blocks[t * buckets : (t + 1) * buckets], 0.0)
            rolled = pltpu.roll(block, (129 - (t + 1) * buckets) % 128, 1, stride=1, stride_axis=0)
            gtab[t, pl.ds(first_row + h, 1), :] = jnp.sum(rolled, axis=0, keepdims=True)
    grads = jnp.concatenate(dqs + dks + dvs, axis=1)
    weights = jnp.concatenate([wq_ref[...], wk_ref[...], wv_ref[...]], axis=1)
    dn[...] += dg(grads, weights, 1, 1)
    gp[step] = dg(n1t[...], grads, 1, 0).astype(BF)
    for i in range(6):
        pl.when(step == i)(functools.partial(slot_end, i))

    @pl.when(step == pl.num_programs(0) - 1)
    def _():
        x = x_ref[...].astype(F32)
        inverse = lax.rsqrt(jnp.mean(x * x, axis=-1, keepdims=True) + EPS)
        normed = x * inverse
        total = dn[...]
        grad_gain = jnp.sum(total * normed, axis=0, keepdims=True)
        inner = total * gain_ref[...]
        added = inverse * (inner - normed * jnp.mean(inner * normed, axis=-1, keepdims=True))
        gin[...] = (dh_ref[...] + added).astype(BF)
        lines = width // 128
        for j in range(lines):
            lane = slice(j * 128, (j + 1) * 128)
            sums[0, j : j + 1, :] = grad_gain[:, lane]
            sums[0, lines + j : lines + j + 1, :] = ggf_ref[:, lane]
        sums[0, 2 * lines : 16, :] = jnp.zeros((16 - 2 * lines, 128), F32)
        line = lax.broadcasted_iota(jnp.int32, (128, 128), 0)
        lane = lax.broadcasted_iota(jnp.int32, (128, 128), 1)
        shift = jnp.where(lane < 64, lane, lane - 128)
        bucket = jnp.clip(-shift, -(buckets // 2), buckets // 2 - 1) + buckets // 2
        table = jnp.zeros((16, 128), F32)
        for t in range(3):
            pick = jnp.where(line == bucket + t * buckets, 1.0, 0.0)
            table = table + lax.dot_general(
                gtab[t], pick, (((1,), (1,)), ((), ())),
                precision=lax.Precision.HIGHEST, preferred_element_type=F32,
            )
        sums[0, 16:32, :] = table
        hops = bits + 1
        hop = None
        count = 0

        def small_hop():
            nonlocal hop, count
            if hop is not None:
                hop.wait_recv()
                k = count
                if k == 1:
                    sums[1, 0:16] = sums[0, 0:16] + got[0, 0:16]
                    sums[1, 16:24] = sums[0, 16:24] + got[0, 24:32]
                    sums[1, 24:32] = jnp.zeros((8, 128), F32)
                else:
                    sums[k] = sums[k - 1] + got[k - 1]
                hop = None
            if count < hops:
                flips = dict(mp_flip=1) if count == 0 else dict(dp_flip=1 << (count - 1))
                k = count
                hop = links.remote(lambda: sums.at[k], lambda: got.at[k], **flips)
                hop.start()
                started.append(hop)
                count += 1

        started = []
        small_hop()
        gin_away.start()
        gin_home.start()
        join_own(2)
        each(ff[0], "start_back_c")
        each(ff[1], "start_back_x")
        each(ff[2], "start_back")
        wo.start_back_x()
        pairs[1].start_z(lambda: ryp.at[1])
        pairs[0].start_back()
        small_hop()
        pairs[2].start_z(lambda: ryp.at[2])
        pairs[0].start_back_x()
        each(ff[1], "start_back_c")
        each(ff[2], "start_back1")
        pairs[1].start_back()
        wo.start_back_c()
        small_hop()
        pairs[2].start_back()
        each(ff[2], "start_back_x")
        pairs[1].start_back_x()
        pairs[0].start_back_c()
        small_hop()
        pairs[2].start_back_x()
        each(ff[2], "start_back_c")
        pairs[1].start_back_c()
        small_hop()
        pairs[2].start_back_c()
        while count < hops or hop is not None:
            small_hop()
        small[...] = sums[hops]
        y_away.wait_recv()
        gin_away.wait_recv()
        for unit in units:
            unit.end()
        for copy in [y_away, gin_away, wo_c, wo_y] + y3 + pair_c + pair_y + started:
            copy.wait_send()
        y_home.wait()
        gin_home.wait()


def backward(p, qt, kv, ot, dot, r, back, hot, x, gain, dh, ggf, wqkv, parts, gwo, y, n_dp, buckets):
    channels, tokens = qt.shape
    width = x.shape[1]
    n_pairs = channels // 128
    half = n_pairs // 2
    chunk = parts[0].shape[1]
    group = 3 * 128
    once = lambda shape: pl.BlockSpec(
        shape, lambda i: (0,) * len(shape), pipeline_mode=pl.Buffered(1)
    )
    pick = lambda i: lax.rem(i + half, n_pairs)
    side = lambda i: pick(i) // half
    place = lambda i: lax.rem(pick(i), half)
    turned = pl.BlockSpec((128, tokens), lambda i: (pick(i), 0))
    column = lambda rows, j, n: pl.BlockSpec(
        (rows, 128), lambda i: (0, side(i) * n * half + j * half + place(i))
    )
    shapes = []
    for k in range(3):
        shapes += [(width, chunk, True), (chunk, width, True)]
    shapes += [(width, group, False)] * 4
    units, far = [], []
    for n, w, deepest in shapes:
        units += [
            pltpu.VMEM((n // 4, w), BF),
            pltpu.VMEM((n // 16, w), BF),
            pltpu.VMEM((n // 8, w) if deepest else (3, n // 16, w), BF),
            pltpu.VMEM((n // 16, w), BF),
        ]
        far.append(pltpu.VMEM((max(n_dp // 16, 1), n // 16, w), BF))
    bits = n_dp.bit_length() - 1
    part_u, part_d = parts[0].shape, parts[1].shape
    copies = 160 + (10 * (n_dp // 16) if n_dp > 16 else 0)
    scratch = [
        pltpu.VMEM((tokens, 128), BF),
        pltpu.VMEM((128, tokens), BF),
        pltpu.VMEM((160, tokens), BF),
        pltpu.VMEM((width, tokens), BF),
        pltpu.VMEM((tokens, width), F32),
        pltpu.VMEM((3, 16, 128), F32),
        pltpu.VMEM((6, width, group), BF),
        pltpu.VMEM((6, width // 2, group), BF),
        pltpu.VMEM((3, width // 2, group), BF),
        pltpu.VMEM((tokens, width), BF),
        pltpu.VMEM(part_u, BF),
        pltpu.VMEM(part_d, BF),
        pltpu.VMEM(part_u, BF),
        pltpu.VMEM(part_d, BF),
        pltpu.VMEM(part_u, BF),
        pltpu.VMEM(part_d, BF),
        pltpu.VMEM(part_u, BF),
        pltpu.VMEM(part_d, BF),
        pltpu.VMEM((width // 2, width), BF),
        pltpu.VMEM((width // 2, width), BF),
        pltpu.VMEM((width // 2, width // 2), BF),
        pltpu.VMEM((bits + 2, 32, 128), F32),
        pltpu.VMEM((bits + 2, 32, 128), F32),
    ]
    scratch += units
    if n_dp > 16:
        scratch += far
    scratch += [pltpu.SemaphoreType.DMA((copies,))] * 2
    return pl.pallas_call(
        functools.partial(back_kernel, n_dp=n_dp, buckets=buckets),
        grid=(n_pairs,),
        in_specs=[
            pl.BlockSpec((2, tokens, tokens), lambda i: (pick(i), 0, 0)),
            turned,
            column(tokens, 0, 2),
            column(tokens, 1, 2),
            turned,
            turned,
            pl.BlockSpec((1, 2, tokens), lambda i: (pick(i), 0, 0)),
            once((96, tokens)),
            once((tokens, 128)),
            once((tokens, width)),
            once((1, width)),
            once((tokens, width)),
            once((1, width)),
            column(width, 0, 3),
            column(width, 1, 3),
            column(width, 2, 3),
        ]
        + [ANY] * 10,
        out_specs=[ANY] * 6 + [once((32, 128))],
        out_shape=[
            SHAPE((2, tokens // 2, width), BF),
            SHAPE((2, tokens // 2, width), BF),
            SHAPE((3, width, group), BF),
            SHAPE((width, group), BF),
            SHAPE((width, 3 * chunk), BF),
            SHAPE((3 * chunk, width), BF),
            SHAPE((32, 128), F32),
        ],
        scratch_shapes=scratch,
        compiler_params=params(60, collective_id=5, has_side_effects=True),
        name="backward",
    )(p, qt, kv, kv, ot, dot, r, back, hot, x, gain, dh, ggf, wqkv, wqkv, wqkv, *parts, gwo, y)


def local(
    n_dp, inputs, roi, cotangent, doc_lengths, live_mask, bucket_cells,
    gain_attn, gain_ffn, w_query, w_key, w_value, w_out, w_up, w_down, tables,
):
    rows, width = inputs.shape[1], inputs.shape[2]
    tokens = 2 * rows
    third = w_query.shape[1]
    heads = third // HDIM
    buckets = tables.shape[1]
    tab = jnp.pad(
        tables.transpose(2, 0, 1).reshape(heads, 3 * buckets), ((0, 2), (0, 128 - 3 * buckets))
    )
    ga, gf = gain_attn.reshape(1, width), gain_ffn.reshape(1, width)
    x, tabo, wqkv, qt, kv, upo = entry(
        inputs, roi, tab, ga, w_query, w_key, w_value, w_up
    )
    p, mixt, r, hot, back, dyo, woo, upo, dno = attend(
        doc_lengths, live_mask.reshape(2, 1, tokens), bucket_cells, tab, tabo, qt, kv,
        cotangent, w_out, w_up, w_down, upo, buckets,
    )
    y, gwo, dh, dmt, gain_f, *parts = middle(
        x, mixt, w_out, woo, cotangent, dyo, gf, w_up, upo, w_down, dno
    )
    yret, gret, fqkv, fwo, fup, fdn, small = backward(
        p, qt, kv, mixt, dmt, r, back, hot, x, ga, dh, gain_f, wqkv, parts, gwo, y, n_dp, buckets
    )
    lines = width // 128
    out = inputs.astype(F32) + roi.astype(F32) + yret.astype(F32)
    grad_in = cotangent.astype(F32) + gret.astype(F32)
    table_out = small[16 : 16 + heads, : 3 * buckets].reshape(heads, 3, buckets).transpose(1, 2, 0)
    gq, gk, gv = (
        jnp.concatenate([fqkv[k, :, j * 128 : (j + 1) * 128] for k in range(3)], axis=1).astype(F32)
        for j in range(3)
    )
    return (
        out,
        grad_in,
        small[0:lines].reshape(width),
        small[lines : 2 * lines].reshape(width),
        gq,
        gk,
        gv,
        fwo.T.astype(F32),
        fup.astype(F32),
        fdn.astype(F32),
        table_out,
    )


def solution(mesh):
    n_dp = mesh.shape["dp"]
    rows = P(None, ("dp", "mp"), None)
    columns, lines = P(None, "mp"), P("mp", None)
    tables = P(None, None, "mp")
    return jax.shard_map(
        functools.partial(local, n_dp),
        mesh=mesh,
        in_specs=(
            rows, rows, rows, P(None, "dp", None), P(None, "dp"), P(None, None, "dp"),
            P(), P(), columns, columns, columns, lines, columns, lines, tables,
        ),
        out_specs=(
            rows, rows, P(), P(), columns, columns, columns, lines, columns, lines, tables,
        ),
        check_vma=False,
    )
```

profile of v0, /device:TPU:0, one launch (start us, length us, event | category | flops | bytes accessed | tf_op | source)
XLA Modules:
  0.0 271.2 jit_solution(3034225559692559557)
XLA Ops:
  0.6 1.3 reshape.45.gain.gain_ref
  1.9 1.3 reshape.46.gain_ref
  3.2 1.3 reshape.43.live
  4.5 0.7 copy.27
  5.2 0.1 reshape.44
  5.3 0.6 pad.4.tab
  5.9 1.4 copy.28.cells
  7.2 39.4 %entry.1 = (bf16[1024,768]{1,0:T(8,128)(2,1)}, f32[8,128]{1,0:T(8,128)}, bf16[768,2304]{1,0:T(8,128)(2,1)}, bf16[768,1024]{1,0:T(8,128)(2,1)}, bf16[1024,1536]{1,0:T(8,128)(2,1)}, /*index=5*/bf16[768,1536]{1,0:T(8,128)(2,1)}) custom-call(bf16[2,512,768]{2,1,0:T(8,128)(2,1)} %inp.1, bf16[2,512,768]{2,1,0:T(8,128)(2,1)} %roi.1, f32[8,128]{1,0:T(8,128)} %pad.4.tab, ...), custom_call_target="tpu_custom_call" | custom-call | tf_op jit(solution)/shard_map/entry/pallas_call | solution.py:205
  46.7 40.9 %attend.1 = (bf16[12,1024,1024]{2,1,0:T(8,128)(2,1)}, bf16[768,1024]{1,0:T(8,128)(2,1)}, f32[6,2,1024]{2,1,0:T(2,128)}, bf16[1024,128]{1,0:T(8,128)(2,1)}, bf16[...) custom-call(s32[2,1,8]{2,1,0:T(1,128)} %lengths.1, ...), custom_call_target="tpu_custom_call", output_to_operand_aliasing={{7}: (12, {})} | custom-call | tf_op jit(solution)/shard_map/attend/pallas_call | solution.py:387
  87.6 57.1 %middle.1 = (bf16[1024,768]{1,0:T(8,128)(2,1)}, bf16[768,768]{1,0:T(8,128)(2,1)}, f32[1024,768]{1,0:T(8,128)}, bf16[768,1024]{1,0:T(8,128)(2,1)}, f32[1,768]{1,0...) custom-call(bf16[1024,768]{1,0:T(8,128)(2,1)} %get-tuple-element.52., ...), custom_call_target="tpu_custom_call" | custom-call | tf_op jit(solution)/shard_map/middle/pallas_call | solution.py:580
  144.7 107.2 %backward.1 = (bf16[2,512,768]{2,1,0:T(8,128)(2,1)}, bf16[2,512,768]{2,1,0:T(8,128)(2,1)}, bf16[3,768,384]{2,1,0:T(8,128)(2,1)}, bf16[768,384]{1,0:T(8,128)(2,1)...) custom-call(bf16[12,1024,1024]{2,1,0:T(8,128)(2,1)} %get-tuple-element.50.p_ref, ...), custom_call_target="tpu_custom_call" | custom-call | tf_op jit(solution)/shard_map/backward/pallas_call | solution.py:1094
  251.9 0.7 slice.47
  252.6 1.3 slice_bitcast_fusion.9
  254.0 0.1 reshape.49
  254.0 0.6 copy.32
  254.6 1.1 convert_bitcast_fusion
  255.8 0.0 copy-start.5
  255.8 1.4 copy.30
  257.2 0.4 copy-done.5
  257.6 0.0 copy-start.6
  257.6 0.0 copy-start.7
  257.6 0.3 slice_bitcast_fusion.2
  258.0 0.0 copy-start.2
  258.0 1.1 maximum_convert_fusion.2
  259.1 0.0 copy-start
  259.1 0.0 copy-start.1
  259.1 1.6 maximum_convert_fusion
  260.6 0.0 copy-done.6
  260.6 0.0 copy-done.7
  260.6 0.4 copy-done.2
  261.0 0.8 copy-done
  261.8 0.5 copy-done.1
  262.3 0.0 copy-start.4
  262.3 3.5 %convert_add_fusion = (f32[2,512,768]{2,1,0:T(8,128)}, f32[2,512,768]{2,1,0:T(8,128)}) fusion(bf16[2,512,768]{2,1,0:T(8,128)(2,1)S(1)} %copy-done.7, bf16[2,512,768]{2,1,0:T(8,128)(2,1)S(1)} %copy-done, bf16[2,512,768]{2,1,0:T(8,128)(2,1)S(1)} %copy-done.6, bf16[2,512,768]{2,1,0:T(8,128)(2,1)S(1)} %copy-done.2, bf16[2,512,768]{2,1,0:T(8,128)(2,1)S(1)} %copy-done.1), kind=kLoop, calls=%fused_computation | loop fusion | flops 6291456 | bytes 14155776 | tf_op jit(solution)/shard_map/add | solution.py:1160
  265.8 0.0 copy-done.4
  265.9 0.0 copy-start.3
  265.9 2.8 %convert_element_type.48 = f32[768,1536]{1,0:T(8,128)} convert(bf16[768,1536]{1,0:T(8,128)(2,1)S(1)} %copy-done.4) | non-fusion elementwise | flops 1179648 | bytes 7077888 | tf_op jit(solution)/shard_map/convert_element_type | solution.py:1175
  268.7 0.0 copy-done.3
  268.7 2.5 convert_element_type.49
Async XLA Ops:
  255.8 1.8 copy-start.5
  257.6 3.0 %copy-start.6 = (bf16[2,512,768]{2,1,0:T(8,128)(2,1)S(1)}, bf16[2,512,768]{2,1,0:T(8,128)(2,1)}, u32[]{:S(2)}) copy-start(bf16[2,512,768]{2,1,0:T(8,128)(2,1)} %get-tuple-element.74) | copy-start | bytes 4718596
  257.6 3.0 %copy-start.7 = (bf16[2,512,768]{2,1,0:T(8,128)(2,1)S(1)}, bf16[2,512,768]{2,1,0:T(8,128)(2,1)}, u32[]{:S(2)}) copy-start(bf16[2,512,768]{2,1,0:T(8,128)(2,1)} %get-tuple-element.75) | copy-start | bytes 4718596
  258.0 3.0 %copy-start.2 = (bf16[2,512,768]{2,1,0:T(8,128)(2,1)S(1)}, bf16[2,512,768]{2,1,0:T(8,128)(2,1)}, u32[]{:S(2)}) copy-start(bf16[2,512,768]{2,1,0:T(8,128)(2,1)} %roi.1) | copy-start | bytes 4718596
  259.1 2.8 %copy-start = (bf16[2,512,768]{2,1,0:T(8,128)(2,1)S(1)}, bf16[2,512,768]{2,1,0:T(8,128)(2,1)}, u32[]{:S(2)}) copy-start(bf16[2,512,768]{2,1,0:T(8,128)(2,1)} %cot.3) | copy-start | bytes 4718596
  259.1 3.2 %copy-start.1 = (bf16[2,512,768]{2,1,0:T(8,128)(2,1)S(1)}, bf16[2,512,768]{2,1,0:T(8,128)(2,1)}, u32[]{:S(2)}) copy-start(bf16[2,512,768]{2,1,0:T(8,128)(2,1)} %inp.1) | copy-start | bytes 4718596
  262.3 3.5 %copy-start.4 = (bf16[768,1536]{1,0:T(8,128)(2,1)S(1)}, bf16[768,1536]{1,0:T(8,128)(2,1)}, u32[]{:S(2)}) copy-start(bf16[768,1536]{1,0:T(8,128)(2,1)} %get-tuple-element.79) | copy-start | bytes 7077892
  265.9 2.8 %copy-start.3 = (bf16[1536,768]{1,0:T(8,128)(2,1)S(1)}, bf16[1536,768]{1,0:T(8,128)(2,1)}, u32[]{:S(2)}) copy-start(bf16[1536,768]{1,0:T(8,128)(2,1)} %get-tuple-element.80) | copy-start | bytes 7077892
where the time goes:
time: 272 us; the launch traced here: 271 us
  Pallas kernels  245 us (90%)
  local copies, waits for them, and re-layouts  13.1 us (5%)
  other arithmetic  12.7 us (5%)
    pallas_call x1, Pallas kernels, backward(): pl.pallas_call(functools.partial(back_kernel, n_dp=n_dp, buckets=buckets)...  107 us
    pallas_call x1, Pallas kernels, middle(): pl.pallas_call(middle_kernel, grid=(n,), in_specs=[once((tokens, width)),...  57.1 us
    pallas_call x1, Pallas kernels, attend(): pl.pallas_call(functools.partial(attend_kernel, buckets=buckets), grid=(p...  40.9 us
    pallas_call x1, Pallas kernels, entry(): pl.pallas_call(entry_kernel, out_shape=[SHAPE((tokens, width), BF), SHAPE...  39.4 us

commit v1 on v0

--- a/solution.py
+++ b/solution.py
@@ -115,7 +115,7 @@
 
 
 def entry_kernel(
-    inp, roi, tab, gain, wq, wk, wv, wup,
+    inp, roi, tab, gains, wq, wk, wv, wup,
     xf, tabo, wqkv, qt, kv, upo,
     sent, n1, send, recv,
 ):
@@ -156,7 +156,7 @@
     def normalise(where):
         x = xf[where].astype(F32)
         inverse = lax.rsqrt(jnp.mean(x * x, axis=-1, keepdims=True) + EPS)
-        n1[where] = (x * inverse * gain[...]).astype(BF)
+        n1[where] = (x * inverse * gains[0:1]).astype(BF)
 
     own = rows_at(m * rows, rows, rows)
     xf[own] = (inp[m].astype(F32) + roi[m].astype(F32)).astype(BF)
@@ -226,7 +226,7 @@
 
 
 def attend_kernel(
-    lengths, live, cells, tab, tabo, qt_ref, k_ref, v_ref, cot, wo, wup, wdn, upo_in,
+    lengths, marks, tab, tabo, qt_ref, k_ref, v_ref, cot, wo, wup, wdn, upo_in,
     p_ref, o_ref, r_ref, hot_ref, back_ref, dyo, woo, upo, dno,
     kx, qx, vx, mask, mats, hott_ref, send, recv, *, buckets,
 ):
@@ -249,16 +249,21 @@
     out = functools.partial(block, woo)
     dpiece, opiece = hidden // 8, inner // 8
     quarter = core * 4 + deep * 2
-    down_y = links.remote(
-        wdn.at[rows_at(quarter * dpiece, 2 * dpiece, dpiece)], down(quarter, 2), mp_flip=1
-    )
+    down_y = [
+        links.remote(
+            wdn.at[rows_at((quarter + j) * dpiece, dpiece, dpiece)], down(quarter + j, 1), mp_flip=1
+        )
+        for j in range(2)
+    ]
     out_y = links.remote(wo.at[rows_at(place * opiece, opiece, opiece)], out(place, 1), mp_flip=1)
     dy_y = links.remote(cot.at[1 - m], dyo, mp_flip=1)
     up_z = links.remote(up(place, 1), up(place, 1), dp_flip=4)
     pair = core * 4 + cross * 2
     up_x = links.remote(up(pair, 2), up(pair, 2), dp_flip=2)
     up_c = links.remote(up(core * 4, 4), up(core * 4, 4), dp_flip=1)
-    down_z = links.remote(down(quarter, 2), down(quarter, 2), dp_flip=4)
+    down_z = [
+        links.remote(down(quarter + j, 1), down(quarter + j, 1), dp_flip=4) for j in range(2)
+    ]
     down_c = links.remote(down(core * 4, 4), down(core * 4, 4), dp_flip=1)
     out_z = links.remote(out(place, 1), out(place, 1), dp_flip=4)
     out_x = links.remote(out(pair, 2), out(pair, 2), dp_flip=2)
@@ -267,21 +272,28 @@
     def slot0():
         links.barrier(((0, 1), (1, 0), (2, 0), (4, 0)))
         up_z.start()
-        down_y.start()
+        down_y[0].start()
         out_y.start()
-        dy_y.start()
 
     def slot4():
         up_z.wait_recv()
         up_x.start()
 
+    def slot2():
+        down_y[1].start()
+
+    def slot5():
+        down_y[0].wait_recv()
+        down_z[0].start()
+
     def slot6():
+        dy_y.start()
         out_y.wait_recv()
         out_z.start()
 
     def slot7():
-        down_y.wait_recv()
-        down_z.start()
+        down_y[1].wait_recv()
+        down_z[1].start()
 
     def slot9():
         out_z.wait_recv()
@@ -294,14 +306,15 @@
         out_c.start()
 
     def last():
-        down_z.wait_recv()
+        down_z[0].wait_recv()
+        down_z[1].wait_recv()
         down_c.start()
         for copy in (dy_y, up_c, out_c, down_c):
             copy.wait_recv()
-        for copy in (down_y, out_y, dy_y, up_z, up_x, up_c, down_z, down_c, out_z, out_x, out_c):
+        for copy in (*down_y, out_y, dy_y, up_z, up_x, up_c, *down_z, down_c, out_z, out_x, out_c):
             copy.wait_send()
 
-    slots = {0: slot0, 4: slot4, 6: slot6, 7: slot7, 9: slot9, 11: slot11}
+    slots = {0: slot0, 1: slot2, 4: slot4, 5: slot5, 6: slot6, 7: slot7, 9: slot9, 11: slot11}
 
     @pl.when(step == 0)
     def _():
@@ -309,7 +322,7 @@
         vx[64:80, :] = jnp.ones((16, tokens), BF)
         lane = lax.broadcasted_iota(jnp.int32, (buckets, tokens), 0)
         for t in range(3):
-            row = cells[m, t : t + 1, :]
+            row = marks[m, t + 1 : t + 2, :]
             hott_ref[t * buckets : (t + 1) * buckets, :] = jnp.where(row == lane, 1.0, 0.0).astype(BF)
             mirror = jnp.where(row == buckets - 1 - lane, 1.0, 0.0).astype(BF)
             back_ref[t * buckets : (t + 1) * buckets, :] = mirror
@@ -328,7 +341,7 @@
             end = end + lengths[m, 0, i]
             seg_row = seg_row + jnp.where(row_ids >= end, 1, 0)
             seg_col = seg_col + jnp.where(col_ids >= end, 1, 0)
-        live_row = live[m].astype(F32)
+        live_row = marks[m, 0:1, :].astype(F32)
         live_col = jnp.broadcast_to(live_row, (8, tokens)).T[:, 0:1]
         code = jnp.where(live_col == 1.0, seg_col, -1)
         allowed = (code == seg_row) | (col_ids == row_ids)
@@ -377,7 +390,7 @@
     pl.when(step == pl.num_programs(0) - 1)(last)
 
 
-def attend(lengths, live, cells, tab, tabo, qt, kv, cot, wo, wup, wdn, upo, buckets):
+def attend(lengths, marks, tab, tabo, qt, kv, cot, wo, wup, wdn, upo, buckets):
     channels, tokens = qt.shape
     width, hidden = wup.shape
     inner = wo.shape[0]
@@ -389,8 +402,7 @@
         grid=(pairs,),
         in_specs=[
             pl.BlockSpec(memory_space=pltpu.SMEM),
-            whole(live.shape),
-            whole(cells.shape),
+            whole(marks.shape),
             whole(tab.shape),
             whole(tabo.shape),
             pl.BlockSpec((128, tokens), lambda i: (i, 0)),
@@ -417,7 +429,7 @@
             SHAPE((width, hidden), BF),
             SHAPE((hidden, width), BF),
         ],
-        input_output_aliases={12: 7},
+        input_output_aliases={11: 7},
         scratch_shapes=[
             pltpu.VMEM((tokens, 256), BF),
             pltpu.VMEM((256, tokens), BF),
@@ -430,11 +442,11 @@
         ],
         compiler_params=params(58, collective_id=3, has_side_effects=True),
         name="attend",
-    )(lengths, live, cells, tab, tabo, qt, kv, kv, cot, wo, wup, wdn, upo)
+    )(lengths, marks, tab, tabo, qt, kv, kv, cot, wo, wup, wdn, upo)
 
 
 def middle_kernel(
-    x_ref, mixt_ref, wo_in, woo_in, cot, dyo, gain_ref, wup_in, upo_in, wdn_in, dno_in,
+    x_ref, mixt_ref, wo_in, woo_in, cot, dyo, gains, wup_in, upo_in, wdn_in, dno_in,
     y_ref, gwo_ref, dh_ref, dmt_ref, gg_ref,
     sum1u, sum1d, sum2u, sum2d, own3u, own3d, far3u, far3d,
     h1, n2, n2t, yacc, dn, wo_ref, dy_ref, gu, gd, rcu, rcd, ryu, ryd, send, recv,
@@ -496,7 +508,7 @@
         h1[...] = h
         yacc[...] = added
         inverse = lax.rsqrt(jnp.mean(h * h, axis=-1, keepdims=True) + EPS)
-        normed = (h * inverse * gain_ref[...]).astype(BF)
+        normed = (h * inverse * gains[1:2]).astype(BF)
         n2[...] = normed
         n2t[...] = normed.T
         dn[...] = jnp.zeros_like(dn)
@@ -534,7 +546,7 @@
         normed = h * inverse
         grad = dn[...]
         gg_ref[...] = jnp.sum(grad * normed, axis=0, keepdims=True)
-        inner = grad * gain_ref[...]
+        inner = grad * gains[1:2]
         added = inverse * (inner - normed * jnp.mean(inner * normed, axis=-1, keepdims=True))
         dh_ref[...] = added
         y_ref[...] = yacc[...].astype(BF)
@@ -587,7 +599,7 @@
             once(woo.shape),
             once(cot.shape),
             once(dyo.shape),
-            once((1, width)),
+            once((2, width)),
             pl.BlockSpec((width, chunk), lambda i: (0, late(i))),
             pl.BlockSpec((width, chunk), lambda i: (0, early(i))),
             pl.BlockSpec((chunk, width), lambda i: (late(i), 0)),
@@ -733,7 +745,7 @@
 
 def back_kernel(
     p_ref, qt_ref, k_ref, v_ref, ot_ref, dot_ref, r_ref, back_ref, hot_ref,
-    x_ref, gain_ref, dh_ref, ggf_ref, wq_ref, wk_ref, wv_ref,
+    x_ref, gains, dh_ref, ggf_ref, wq_ref, wk_ref, wv_ref,
     sum1u, sum1d, sum2u, sum2d, own3u, own3d, far3u, far3d, gwo, y,
     yret, gret, fqkv, fwo, fup, fdn, small,
     vx, dox, kht, n1t, dn, gtab, gp, rcp, ryp, gin,
@@ -894,7 +906,7 @@
         dox[64:128, :] = jnp.zeros((64, tokens), BF)
         x = x_ref[...].astype(F32)
         inverse = lax.rsqrt(jnp.mean(x * x, axis=-1, keepdims=True) + EPS)
-        n1t[...] = (x * inverse * gain_ref[...]).astype(BF).T
+        n1t[...] = (x * inverse * gains[0:1]).astype(BF).T
         dn[...] = jnp.zeros_like(dn)
         gtab[...] = jnp.zeros_like(gtab)
 
@@ -942,7 +954,7 @@
         normed = x * inverse
         total = dn[...]
         grad_gain = jnp.sum(total * normed, axis=0, keepdims=True)
-        inner = total * gain_ref[...]
+        inner = total * gains[0:1]
         added = inverse * (inner - normed * jnp.mean(inner * normed, axis=-1, keepdims=True))
         gin[...] = (dh_ref[...] + added).astype(BF)
         lines = width // 128
@@ -1105,7 +1117,7 @@
             once((96, tokens)),
             once((tokens, 128)),
             once((tokens, width)),
-            once((1, width)),
+            once((2, width)),
             once((tokens, width)),
             once((1, width)),
             column(width, 0, 3),
@@ -1141,19 +1153,20 @@
     tab = jnp.pad(
         tables.transpose(2, 0, 1).reshape(heads, 3 * buckets), ((0, 2), (0, 128 - 3 * buckets))
     )
-    ga, gf = gain_attn.reshape(1, width), gain_ffn.reshape(1, width)
+    marks = jnp.concatenate([live_mask[:, None, :], bucket_cells], axis=1)
+    gains = jnp.stack([gain_attn, gain_ffn])
     x, tabo, wqkv, qt, kv, upo = entry(
-        inputs, roi, tab, ga, w_query, w_key, w_value, w_up
+        inputs, roi, tab, gains, w_query, w_key, w_value, w_up
     )
     p, mixt, r, hot, back, dyo, woo, upo, dno = attend(
-        doc_lengths, live_mask.reshape(2, 1, tokens), bucket_cells, tab, tabo, qt, kv,
+        doc_lengths, marks, tab, tabo, qt, kv,
         cotangent, w_out, w_up, w_down, upo, buckets,
     )
     y, gwo, dh, dmt, gain_f, *parts = middle(
-        x, mixt, w_out, woo, cotangent, dyo, gf, w_up, upo, w_down, dno
+        x, mixt, w_out, woo, cotangent, dyo, gains, w_up, upo, w_down, dno
     )
     yret, gret, fqkv, fwo, fup, fdn, small = backward(
-        p, qt, kv, mixt, dmt, r, back, hot, x, ga, dh, gain_f, wqkv, parts, gwo, y, n_dp, buckets
+        p, qt, kv, mixt, dmt, r, back, hot, x, gains, dh, gain_f, wqkv, parts, gwo, y, n_dp, buckets
     )
     lines = width // 128
     out = inputs.astype(F32) + roi.astype(F32) + yret.astype(F32)

time: 272 us -> 268 us (0.985)
  Pallas kernels: 245 us -> 242 us
    reshape x3 -> x0, local copies, waits for them, and re-layouts: 3.83 us -> none  [the longest x2 2.53 us: local(): ga, gf = (gain_attn.reshape(1, width), gain_ffn.reshape(1, width))]
where the time goes in v1:
time: 268 us
  Pallas kernels  242 us (90%)
  other arithmetic  13.9 us (5%)
  local copies, waits for them, and re-layouts  10.8 us (4%)
    pallas_call x1, Pallas kernels, backward(): pl.pallas_call(functools.partial(back_kernel, n_dp=n_dp, buckets=buckets)...  107 us
    pallas_call x1, Pallas kernels, middle(): pl.pallas_call(middle_kernel, grid=(n,), in_specs=[once((tokens, width)),...  57.1 us
    pallas_call x1, Pallas kernels, entry(): pl.pallas_call(entry_kernel, out_shape=[SHAPE((tokens, width), BF), SHAPE...  39.4 us
    pallas_call x1, Pallas kernels, attend(): pl.pallas_call(functools.partial(attend_kernel, buckets=buckets), grid=(p...  38.8 us

profile of v1, /device:TPU:0, one launch (start us, length us, event | category | flops | bytes accessed | tf_op | source)
XLA Modules:
  0.0 267.7 jit_solution(10079003066842155922)
XLA Ops:
  0.6 0.7 stack.9
  1.3 0.7 stack.10
  2.0 0.6 pad_maximum_fusion.gains
  2.6 0.7 broadcast_in_dim.3
  3.3 0.7 copy.28
  4.0 0.1 reshape.34
  4.1 0.6 pad.4.tab
  4.7 0.8 copy.27
  5.5 0.6 pad_add_fusion.marks
  6.1 39.4 %entry.1 = (bf16[1024,768]{1,0:T(8,128)(2,1)}, f32[8,128]{1,0:T(8,128)}, bf16[768,2304]{1,0:T(8,128)(2,1)}, bf16[768,1024]{1,0:T(8,128)(2,1)}, bf16[1024,1536]{1,0:T(8,128)(2,1)}, /*index=5*/bf16[768,1536]{1,0:T(8,128)(2,1)}) custom-call(bf16[2,512,768]{2,1,0:T(8,128)(2,1)} %inp.1, bf16[2,512,768]{2,1,0:T(8,128)(2,1)} %roi.1, f32[8,128]{1,0:T(8,128)} %pad.4.tab, ...), custom_call_target="tpu_custom_call" | custom-call | tf_op jit(solution)/shard_map/entry/pallas_call | solution.py:205
  45.6 38.8 %attend.1 = (bf16[12,1024,1024]{2,1,0:T(8,128)(2,1)}, bf16[768,1024]{1,0:T(8,128)(2,1)}, f32[6,2,1024]{2,1,0:T(2,128)}, bf16[1024,128]{1,0:T(8,128)(2,1)}, bf16[...) custom-call(s32[2,1,8]{2,1,0:T(1,128)} %lengths.1, ...), custom_call_target="tpu_custom_call", output_to_operand_aliasing={{7}: (11, {})} | custom-call | tf_op jit(solution)/shard_map/attend/pallas_call | solution.py:400
  84.4 57.1 %middle.1 = (bf16[1024,768]{1,0:T(8,128)(2,1)}, bf16[768,768]{1,0:T(8,128)(2,1)}, f32[1024,768]{1,0:T(8,128)}, bf16[768,1024]{1,0:T(8,128)(2,1)}, f32[1,768]{1,0...) custom-call(bf16[1024,768]{1,0:T(8,128)(2,1)} %get-tuple-element.52., ...), custom_call_target="tpu_custom_call" | custom-call | tf_op jit(solution)/shard_map/middle/pallas_call | solution.py:592
  141.5 106.9 %backward.1 = (bf16[2,512,768]{2,1,0:T(8,128)(2,1)}, bf16[2,512,768]{2,1,0:T(8,128)(2,1)}, bf16[3,768,384]{2,1,0:T(8,128)(2,1)}, bf16[768,384]{1,0:T(8,128)(2,1)...) custom-call(bf16[12,1024,1024]{2,1,0:T(8,128)(2,1)} %get-tuple-element.50.p_ref, ...), custom_call_target="tpu_custom_call" | custom-call | tf_op jit(solution)/shard_map/backward/pallas_call | solution.py:1106
  248.4 0.7 slice.47
  249.1 1.3 slice_bitcast_fusion.9
  250.4 0.1 reshape.37
  250.5 0.6 copy.32
  251.1 1.1 convert_bitcast_fusion
  252.3 0.0 copy-start.5
  252.3 1.4 copy.30
  253.7 0.4 copy-done.5
  254.1 0.0 copy-start.6
  254.1 0.0 copy-start.7
  254.1 0.3 slice_bitcast_fusion.2
  254.4 0.0 copy-start.2
  254.4 1.1 maximum_convert_fusion.2
  255.5 0.0 copy-start
  255.5 0.0 copy-start.1
  255.5 1.6 maximum_convert_fusion
  257.1 0.0 copy-done.6
  257.1 0.0 copy-done.7
  257.1 0.4 copy-done.2
  257.5 0.8 copy-done
  258.3 0.5 copy-done.1
  258.8 0.0 copy-start.4
  258.8 3.5 %convert_add_fusion = (f32[2,512,768]{2,1,0:T(8,128)}, f32[2,512,768]{2,1,0:T(8,128)}) fusion(bf16[2,512,768]{2,1,0:T(8,128)(2,1)S(1)} %copy-done.7, bf16[2,512,768]{2,1,0:T(8,128)(2,1)S(1)} %copy-done, bf16[2,512,768]{2,1,0:T(8,128)(2,1)S(1)} %copy-done.6, bf16[2,512,768]{2,1,0:T(8,128)(2,1)S(1)} %copy-done.2, bf16[2,512,768]{2,1,0:T(8,128)(2,1)S(1)} %copy-done.1), kind=kLoop, calls=%fused_computation | loop fusion | flops 6291456 | bytes 14155776 | tf_op jit(solution)/shard_map/add | solution.py:1173
  262.3 0.0 copy-done.4
  262.3 0.0 copy-start.3
  262.3 2.8 %convert_element_type.48 = f32[768,1536]{1,0:T(8,128)} convert(bf16[768,1536]{1,0:T(8,128)(2,1)S(1)} %copy-done.4) | non-fusion elementwise | flops 1179648 | bytes 7077888 | tf_op jit(solution)/shard_map/convert_element_type | solution.py:1188
  265.1 0.0 copy-done.3
  265.1 2.5 convert_element_type.49
Async XLA Ops:
  252.3 1.8 copy-start.5
  254.1 3.0 %copy-start.6 = (bf16[2,512,768]{2,1,0:T(8,128)(2,1)S(1)}, bf16[2,512,768]{2,1,0:T(8,128)(2,1)}, u32[]{:S(2)}) copy-start(bf16[2,512,768]{2,1,0:T(8,128)(2,1)} %get-tuple-element.74) | copy-start | bytes 4718596
  254.1 3.0 %copy-start.7 = (bf16[2,512,768]{2,1,0:T(8,128)(2,1)S(1)}, bf16[2,512,768]{2,1,0:T(8,128)(2,1)}, u32[]{:S(2)}) copy-start(bf16[2,512,768]{2,1,0:T(8,128)(2,1)} %get-tuple-element.75) | copy-start | bytes 4718596
  254.4 3.0 %copy-start.2 = (bf16[2,512,768]{2,1,0:T(8,128)(2,1)S(1)}, bf16[2,512,768]{2,1,0:T(8,128)(2,1)}, u32[]{:S(2)}) copy-start(bf16[2,512,768]{2,1,0:T(8,128)(2,1)} %roi.1) | copy-start | bytes 4718596
  255.5 2.8 %copy-start = (bf16[2,512,768]{2,1,0:T(8,128)(2,1)S(1)}, bf16[2,512,768]{2,1,0:T(8,128)(2,1)}, u32[]{:S(2)}) copy-start(bf16[2,512,768]{2,1,0:T(8,128)(2,1)} %cot.3) | copy-start | bytes 4718596
  255.5 3.2 %copy-start.1 = (bf16[2,512,768]{2,1,0:T(8,128)(2,1)S(1)}, bf16[2,512,768]{2,1,0:T(8,128)(2,1)}, u32[]{:S(2)}) copy-start(bf16[2,512,768]{2,1,0:T(8,128)(2,1)} %inp.1) | copy-start | bytes 4718596
  258.8 3.5 %copy-start.4 = (bf16[768,1536]{1,0:T(8,128)(2,1)S(1)}, bf16[768,1536]{1,0:T(8,128)(2,1)}, u32[]{:S(2)}) copy-start(bf16[768,1536]{1,0:T(8,128)(2,1)} %get-tuple-element.79) | copy-start | bytes 7077892
  262.3 2.8 %copy-start.3 = (bf16[1536,768]{1,0:T(8,128)(2,1)S(1)}, bf16[1536,768]{1,0:T(8,128)(2,1)}, u32[]{:S(2)}) copy-start(bf16[1536,768]{1,0:T(8,128)(2,1)} %get-tuple-element.80) | copy-start | bytes 7077892

commit v2 on v1

--- a/solution.py
+++ b/solution.py
@@ -879,7 +879,6 @@
             each(ff[0], "start_back")
             each(ff[1], "start_z2")
             send_other(2)
-            y_away.start()
             wo_y.wait_recv()
             accumulate(ryw, rcw.at[:, 0:heads_half])
             wo.start_x(ryw)
@@ -889,6 +888,7 @@
             ff_z(2)
             join_own(0)
             wo.start_z(ryw)
+            y_away.start()
         if i == 5:
             each(ff[0], "start_back_x")
             each(ff[1], "start_back1")
@@ -896,6 +896,7 @@
             join_own(1)
             wo.start_back()
             pairs[0].start_z(lambda: ryp.at[0])
+            join_own(2)
 
     @pl.when(step == 0)
     def _():
@@ -1003,7 +1004,6 @@
         small_hop()
         gin_away.start()
         gin_home.start()
-        join_own(2)
         each(ff[0], "start_back_c")
         each(ff[1], "start_back_x")
         each(ff[2], "start_back")

time: 268 us -> 268 us (level)
  no operation moved by 1% of the time
where the time goes in v2:
time: 268 us; the launch traced here: 267 us
  Pallas kernels  242 us (90%)
  other arithmetic  13.9 us (5%)
  local copies, waits for them, and re-layouts  10.8 us (4%)
    pallas_call x1, Pallas kernels, backward(): pl.pallas_call(functools.partial(back_kernel, n_dp=n_dp, buckets=buckets)...  107 us
    pallas_call x1, Pallas kernels, middle(): pl.pallas_call(middle_kernel, grid=(n,), in_specs=[once((tokens, width)),...  57.1 us
    pallas_call x1, Pallas kernels, entry(): pl.pallas_call(entry_kernel, out_shape=[SHAPE((tokens, width), BF), SHAPE...  39.4 us
    pallas_call x1, Pallas kernels, attend(): pl.pallas_call(functools.partial(attend_kernel, buckets=buckets), grid=(p...  38.8 us

profile of v2, /device:TPU:0, one launch (start us, length us, event | category | flops | bytes accessed | tf_op | source)
XLA Modules:
  0.0 267.5 jit_solution(13705632004563341254)
XLA Ops:
  0.6 0.7 stack.9
  1.3 0.7 stack.10
  2.0 0.6 pad_maximum_fusion.gains
  2.6 0.7 broadcast_in_dim.3
  3.3 0.7 copy.28
  4.0 0.1 reshape.34
  4.1 0.6 pad.4.tab
  4.7 0.8 copy.27
  5.5 0.6 pad_add_fusion.marks
  6.1 39.4 %entry.1 = (bf16[1024,768]{1,0:T(8,128)(2,1)}, f32[8,128]{1,0:T(8,128)}, bf16[768,2304]{1,0:T(8,128)(2,1)}, bf16[768,1024]{1,0:T(8,128)(2,1)}, bf16[1024,1536]{1,0:T(8,128)(2,1)}, /*index=5*/bf16[768,1536]{1,0:T(8,128)(2,1)}) custom-call(bf16[2,512,768]{2,1,0:T(8,128)(2,1)} %inp.1, bf16[2,512,768]{2,1,0:T(8,128)(2,1)} %roi.1, f32[8,128]{1,0:T(8,128)} %pad.4.tab, ...), custom_call_target="tpu_custom_call" | custom-call | tf_op jit(solution)/shard_map/entry/pallas_call | solution.py:205
  45.6 38.8 %attend.1 = (bf16[12,1024,1024]{2,1,0:T(8,128)(2,1)}, bf16[768,1024]{1,0:T(8,128)(2,1)}, f32[6,2,1024]{2,1,0:T(2,128)}, bf16[1024,128]{1,0:T(8,128)(2,1)}, bf16[...) custom-call(s32[2,1,8]{2,1,0:T(1,128)} %lengths.1, ...), custom_call_target="tpu_custom_call", output_to_operand_aliasing={{7}: (11, {})} | custom-call | tf_op jit(solution)/shard_map/attend/pallas_call | solution.py:400
  84.4 57.1 %middle.1 = (bf16[1024,768]{1,0:T(8,128)(2,1)}, bf16[768,768]{1,0:T(8,128)(2,1)}, f32[1024,768]{1,0:T(8,128)}, bf16[768,1024]{1,0:T(8,128)(2,1)}, f32[1,768]{1,0...) custom-call(bf16[1024,768]{1,0:T(8,128)(2,1)} %get-tuple-element.52., ...), custom_call_target="tpu_custom_call" | custom-call | tf_op jit(solution)/shard_map/middle/pallas_call | solution.py:592
  141.5 106.7 %backward.1 = (bf16[2,512,768]{2,1,0:T(8,128)(2,1)}, bf16[2,512,768]{2,1,0:T(8,128)(2,1)}, bf16[3,768,384]{2,1,0:T(8,128)(2,1)}, bf16[768,384]{1,0:T(8,128)(2,1)...) custom-call(bf16[12,1024,1024]{2,1,0:T(8,128)(2,1)} %get-tuple-element.50.p_ref, ...), custom_call_target="tpu_custom_call" | custom-call | tf_op jit(solution)/shard_map/backward/pallas_call | solution.py:1106
  248.2 0.7 slice.47
  248.9 1.3 slice_bitcast_fusion.9
  250.2 0.1 reshape.37
  250.3 0.6 copy.32
  250.9 1.1 convert_bitcast_fusion
  252.1 0.0 copy-start.5
  252.1 1.4 copy.30
  253.5 0.4 copy-done.5
  253.9 0.0 copy-start.6
  253.9 0.0 copy-start.7
  253.9 0.3 slice_bitcast_fusion.2
  254.2 0.0 copy-start.2
  254.2 1.1 maximum_convert_fusion.2
  255.3 0.0 copy-start
  255.3 0.0 copy-start.1
  255.3 1.6 maximum_convert_fusion
  256.9 0.0 copy-done.6
  256.9 0.0 copy-done.7
  256.9 0.4 copy-done.2
  257.3 0.8 copy-done
  258.1 0.5 copy-done.1
  258.6 0.0 copy-start.4
  258.6 3.5 %convert_add_fusion = (f32[2,512,768]{2,1,0:T(8,128)}, f32[2,512,768]{2,1,0:T(8,128)}) fusion(bf16[2,512,768]{2,1,0:T(8,128)(2,1)S(1)} %copy-done.7, bf16[2,512,768]{2,1,0:T(8,128)(2,1)S(1)} %copy-done, bf16[2,512,768]{2,1,0:T(8,128)(2,1)S(1)} %copy-done.6, bf16[2,512,768]{2,1,0:T(8,128)(2,1)S(1)} %copy-done.2, bf16[2,512,768]{2,1,0:T(8,128)(2,1)S(1)} %copy-done.1), kind=kLoop, calls=%fused_computation | loop fusion | flops 6291456 | bytes 14155776 | tf_op jit(solution)/shard_map/add | solution.py:1173
  262.1 0.0 copy-done.4
  262.1 0.0 copy-start.3
  262.1 2.8 %convert_element_type.48 = f32[768,1536]{1,0:T(8,128)} convert(bf16[768,1536]{1,0:T(8,128)(2,1)S(1)} %copy-done.4) | non-fusion elementwise | flops 1179648 | bytes 7077888 | tf_op jit(solution)/shard_map/convert_element_type | solution.py:1188
  264.9 0.0 copy-done.3
  264.9 2.5 convert_element_type.49
Async XLA Ops:
  252.1 1.8 copy-start.5
  253.9 3.0 %copy-start.6 = (bf16[2,512,768]{2,1,0:T(8,128)(2,1)S(1)}, bf16[2,512,768]{2,1,0:T(8,128)(2,1)}, u32[]{:S(2)}) copy-start(bf16[2,512,768]{2,1,0:T(8,128)(2,1)} %get-tuple-element.74) | copy-start | bytes 4718596
  253.9 3.0 %copy-start.7 = (bf16[2,512,768]{2,1,0:T(8,128)(2,1)S(1)}, bf16[2,512,768]{2,1,0:T(8,128)(2,1)}, u32[]{:S(2)}) copy-start(bf16[2,512,768]{2,1,0:T(8,128)(2,1)} %get-tuple-element.75) | copy-start | bytes 4718596
  254.2 3.0 %copy-start.2 = (bf16[2,512,768]{2,1,0:T(8,128)(2,1)S(1)}, bf16[2,512,768]{2,1,0:T(8,128)(2,1)}, u32[]{:S(2)}) copy-start(bf16[2,512,768]{2,1,0:T(8,128)(2,1)} %roi.1) | copy-start | bytes 4718596
  255.3 2.8 %copy-start = (bf16[2,512,768]{2,1,0:T(8,128)(2,1)S(1)}, bf16[2,512,768]{2,1,0:T(8,128)(2,1)}, u32[]{:S(2)}) copy-start(bf16[2,512,768]{2,1,0:T(8,128)(2,1)} %cot.3) | copy-start | bytes 4718596
  255.3 3.2 %copy-start.1 = (bf16[2,512,768]{2,1,0:T(8,128)(2,1)S(1)}, bf16[2,512,768]{2,1,0:T(8,128)(2,1)}, u32[]{:S(2)}) copy-start(bf16[2,512,768]{2,1,0:T(8,128)(2,1)} %inp.1) | copy-start | bytes 4718596
  258.6 3.5 %copy-start.4 = (bf16[768,1536]{1,0:T(8,128)(2,1)S(1)}, bf16[768,1536]{1,0:T(8,128)(2,1)}, u32[]{:S(2)}) copy-start(bf16[768,1536]{1,0:T(8,128)(2,1)} %get-tuple-element.79) | copy-start | bytes 7077892
  262.1 2.8 %copy-start.3 = (bf16[1536,768]{1,0:T(8,128)(2,1)S(1)}, bf16[1536,768]{1,0:T(8,128)(2,1)}, u32[]{:S(2)}) copy-start(bf16[1536,768]{1,0:T(8,128)(2,1)} %get-tuple-element.80) | copy-start | bytes 7077892
